TPU v7x, 32 devices: a whole 2x2x4 slice. The times are simulated.
32 devices in a mesh: blk: 8 (over y, x, core), grp: 4 (over z).
Axes of the slice: x: 2, y: 2, z: 4, core: 2. Of those that a mesh axis runs over, the one named last changes fastest.
Arguments:
- depth: float32 [256, 128, 128], P(('blk', 'grp')), may hold values from 0.2 to 1
- cell_dx: float32 [256, 128, 128], P(('blk', 'grp')), may hold values from 0.6 to 1.5
- cell_dy: float32 [256, 128, 128], P(('blk', 'grp')), may hold values from 0.6 to 1.5
- forcing: float32 [256, 128, 128], P(('blk', 'grp')), may hold values from -6 to 6
- land_mask: int32 [256, 128, 128], P(('blk', 'grp')), may hold values 0 or 1
- dest_block: int32 [256], P(('blk', 'grp')), may hold values from -1 to 127, as said below
- source_slot: int32 [128], P(('blk', 'grp')), may hold values from 0 to 255, as said below
- neighbours: int32 [128, 8], P(('blk', 'grp')), may hold values from -1 to 127, as said below
Outputs:
- solution: float32 [128, 128, 128], P(('blk', 'grp'))
- residual: float32 [128, 128, 128], P(('blk', 'grp'))
Inputs may be any that keep to these rules, and one draw needn't show every extreme that they name: `dest_block`: every ocean block is held by exactly one old slot; a block's old and new owners share their index on grp and lie in the same aligned group of four indices on blk. One device's live slots send at most 4 blocks to any one device; in every band some devices hold no block and some have all 8 slots live. `source_slot`: the inverse of dest_block. North and south neighbours lie on devices with the same index on grp; east, north-east and south-east neighbours on the device with the same index on blk and the next index on grp, cyclically; west, north-west and south-west ones on the previous index on grp.
All inputs are finite; a program needn't handle non-finite values. No bound on the sum of `land_mask` on one device may be relied on, other than what follows from the above.
Results may differ from a plain program's by a relative error of at most 0.000034.
Values sent between devices are 32-bit elements; how exact they have to be, the bound alone decides.
A program may use at most 64 MiB of HBM per device.

v0:
```python
import jax
import jax.numpy as jnp
from jax import lax
from jax.sharding import PartitionSpec as P

SWEEPS = 4


tau_mass = 6.0
low_bound = 0.2
high_bound = 1.9


def extended(shard, sides, width):
    for axis, dim in sides:
        size, length = (lax.axis_size(axis), shard.shape[dim])
        up = [(i, (i + 1) % size) for i in range(size)]
        down = [(j, i) for i, j in up]
        last = lax.slice_in_dim(shard, length - width, length, axis=dim)
        first = lax.slice_in_dim(shard, 0, width, axis=dim)
        before = lax.ppermute(last, axis, up)
        after = lax.ppermute(first, axis, down)
        shard = jnp.concatenate([before, shard, after], axis=dim)
    return shard


def partner_2(shard, axis, apart):
    return lax.ppermute(shard, axis, [(i, i ^ 1 << apart) for i in range(lax.axis_size(axis))])


def coefficients(ocean_depth, cell_dx, cell_dy):
    ratio_x = cell_dy / cell_dx
    ratio_y = cell_dx / cell_dy
    coef_x = ocean_depth * ratio_x
    coef_y = ocean_depth * ratio_y
    coef_c = 0.125 * ocean_depth * (ratio_x + ratio_y)
    coef_d = 2.0 * coef_x + 2.0 * coef_y + 4.0 * coef_c + tau_mass * cell_dx * cell_dy
    return (coef_x, coef_y, coef_c, coef_d)


def combine(
    iterate,
    coefs,
    north_row,
    south_row,
    west_col,
    east_col,
    north_west,
    north_east,
    south_west,
    south_east,
):
    coef_x, coef_y, coef_c, coef_d = coefs
    top_pad = jnp.concatenate((north_west[:, None], north_row, north_east[:, None]), axis=1)
    bottom_pad = jnp.concatenate((south_west[:, None], south_row, south_east[:, None]), axis=1)
    middle = jnp.concatenate((west_col[:, :, None], iterate, east_col[:, :, None]), axis=2)
    padded = jnp.concatenate((top_pad[:, None, :], middle, bottom_pad[:, None, :]), axis=1)
    from_north = padded[:, :-2, 1:-1]
    from_south = padded[:, 2:, 1:-1]
    from_west = padded[:, 1:-1, :-2]
    from_east = padded[:, 1:-1, 2:]
    diagonal = padded[:, :-2, :-2] + padded[:, :-2, 2:] + padded[:, 2:, :-2] + padded[:, 2:, 2:]
    return (
        coef_d * iterate
        - coef_x * (from_east + from_west)
        - coef_y * (from_north + from_south)
        - coef_c * diagonal
    )


def apply_operator(iterate, coefs, present, band_index, local_slot):
    width = iterate.shape[2]
    height = iterate.shape[1]
    top_bottom = jnp.stack((iterate[:, 0, :], iterate[:, -1, :]), axis=1)
    band_rows = lax.all_gather(top_bottom, "blk", axis=0, tiled=True)
    packed = jnp.concatenate(
        (iterate[:, 0, :], iterate[:, -1, :], iterate[:, :, 0], iterate[:, :, -1]), axis=1
    )
    beside = extended(packed[None], (("grp", 0),), 1)
    west_side = beside[0]
    east_side = beside[2]
    north_row = jnp.where(present[:, 0, None], band_rows[band_index[:, 0], 1], 0.0)
    south_row = jnp.where(present[:, 1, None], band_rows[band_index[:, 1], 0], 0.0)
    east_col = jnp.where(
        present[:, 2, None], east_side[local_slot[:, 2], 2 * width : 2 * width + height], 0.0
    )
    west_col = jnp.where(
        present[:, 3, None], west_side[local_slot[:, 3], 2 * width + height :], 0.0
    )
    north_east = jnp.where(present[:, 4], east_side[local_slot[:, 4], width], 0.0)
    north_west = jnp.where(present[:, 5], west_side[local_slot[:, 5], 2 * width - 1], 0.0)
    south_east = jnp.where(present[:, 6], east_side[local_slot[:, 6], 0], 0.0)
    south_west = jnp.where(present[:, 7], west_side[local_slot[:, 7], width - 1], 0.0)
    return combine(
        iterate,
        coefs,
        north_row,
        south_row,
        west_col,
        east_col,
        north_west,
        north_east,
        south_west,
        south_east,
    )


def move_blocks(fields, dest_block, source_slot, slot_count):
    blocks = source_slot.shape[0]
    groups = lax.axis_size("grp")
    owner_here = lax.axis_index("blk")
    live = dest_block >= 0
    safe_dest = jnp.where(live, dest_block, 0)
    new_owner = safe_dest // blocks // groups
    new_local = safe_dest % blocks
    partner = jnp.where(live, jnp.bitwise_xor(new_owner, owner_here), 4)

    def place(offset):
        index = jnp.where(partner == offset, new_local, blocks)
        return (
            jnp.zeros((blocks,) + fields.shape[1:], jnp.float32).at[index].set(fields, mode="drop")
        )

    sectioned = partner_2(jnp.stack((place(2), place(3))), "blk", 1)
    paired = partner_2(jnp.stack((place(1), sectioned[1])), "blk", 0)
    arrivals = jnp.stack((place(0), sectioned[0], paired[0], paired[1]))
    anchor = jnp.bitwise_xor(source_slot // slot_count // groups, owner_here)
    which = jnp.where(anchor == 1, 2, jnp.where(anchor == 2, 1, anchor))
    return arrivals[which, jnp.arange(blocks)]


def per_device(depth, cell_dx, cell_dy, forcing, land_mask, dest_block, source_slot, neighbours):
    blocks = source_slot.shape[0]
    slot_count = depth.shape[0]
    groups = lax.axis_size("grp")
    ocean_mask = land_mask.astype(jnp.float32)
    ocean_depth = depth * ocean_mask
    source_old = forcing * ocean_mask
    fields = jnp.stack(coefficients(ocean_depth, cell_dx, cell_dy) + (source_old,), axis=1)
    arrived = move_blocks(fields, dest_block, source_slot, slot_count)
    coefs = (arrived[:, 0], arrived[:, 1], arrived[:, 2], arrived[:, 3])
    source = arrived[:, 4]
    present = neighbours >= 0
    safe_ids = jnp.where(present, neighbours, 0)
    local_slot = safe_ids % blocks
    band_index = safe_ids // blocks // groups * blocks + local_slot
    coef_d = coefs[3]
    scale_alpha = 2.0 / (high_bound - low_bound)
    scale_beta = (high_bound + low_bound) / (high_bound - low_bound)
    scale_gamma = scale_beta / scale_alpha
    relax_weight = 2.0 / scale_gamma
    update = source / (scale_gamma * coef_d)
    solution = update
    residual = source - apply_operator(solution, coefs, present, band_index, local_slot)
    for sweep in range(SWEEPS - 1):
        relax_weight = 1.0 / (scale_gamma - relax_weight / (4.0 * scale_alpha**2))
        update = relax_weight * residual / coef_d + (scale_gamma * relax_weight - 1.0) * update
        solution = solution + update
        residual = source - apply_operator(solution, coefs, present, band_index, local_slot)
    return (solution, residual)


def solution(mesh):
    in_specs = (
        P(("blk", "grp"), None, None),
        P(("blk", "grp"), None, None),
        P(("blk", "grp"), None, None),
        P(("blk", "grp"), None, None),
        P(("blk", "grp"), None, None),
        P(("blk", "grp")),
        P(("blk", "grp")),
        P(("blk", "grp"), None),
    )
    out_specs = (P(("blk", "grp"), None, None), P(("blk", "grp"), None, None))
    return jax.shard_map(
        per_device, mesh=mesh, in_specs=in_specs, out_specs=out_specs, check_vma=False
    )
```

profile of v0, /device:TPU:0, one launch (start us, length us, event | category | flops | bytes accessed | tf_op | source)
XLA Modules:
  0.0 241.4 jit_solution(2032820057156698950)
XLA Ops:
  0.7 1.7 bitcast_dynamic-update-slice_fusion.4
  5.6 3.2 %scatter_fusion.1 = f32[4,5,128,128]{3,2,1,0:T(8,128)} fusion(f32[4,5,128,128]{3,2,1,0:T(8,128)} %broadcast.342.clone.1, s32[8]{0:T(128)S(1)} %get-tuple-element.359, f32[8,5,128,128]{3,2,1,0:T(8,128)S(1)} %copy.232), kind=kCustom, calls=%fused_computation.26 | custom fusion | bytes 7864352 | tf_op jit(solution)/shard_map/scatter | solution.py:121
  10.1 3.3 %scatter_fusion.2 = f32[4,5,128,128]{3,2,1,0:T(8,128)} fusion(f32[4,5,128,128]{3,2,1,0:T(8,128)} %broadcast.342.clone, s32[8]{0:T(128)S(1)} %get-tuple-element.358, f32[8,5,128,128]{3,2,1,0:T(8,128)S(1)} %copy.232), kind=kCustom, calls=%fused_computation.27 | custom fusion | bytes 7864352 | tf_op jit(solution)/shard_map/scatter | solution.py:121
  13.4 3.5 %pad_maximum_fusion.1 = f32[2,4,5,128,128]{4,3,2,1,0:T(8,128)} fusion(f32[1,4,5,128,128]{4,3,2,1,0:T(8,128)} %bitcast.224, f32[1,4,5,128,128]{4,3,2,1,0:T(8,128)} %bitcast.223), kind=kLoop, calls=%fused_computation.38 | loop fusion | flops 655360 | bytes 5242880 | tf_op jit(solution)/shard_map/stack | solution.py:124
  16.9 3.6 %collective-permute-start = (f32[2,4,5,128,128]{4,3,2,1,0:T(8,128)}, f32[2,4,5,128,128]{4,3,2,1,0:T(8,128)}, u32[]{:S(2)}, u32[]{:S(2)}) collective-permute-start(f32[2,4,5,128,128]{4,3,2,1,0:T(8,128)} %pad_maximum_fusion.1), channel_id=1, source_target_pairs={{0,8},{4,12},{8,0},{12,4},{16,24},{20,28},{24,16},{28,20},{1,9},{5... | collective-permute-start | bytes 7864328 | tf_op jit(solution)/shard_map/ppermute | solution.py:28
  21.8 3.8 %scatter_fusion.3 = f32[4,5,128,128]{3,2,1,0:T(8,128)} fusion(f32[4,5,128,128]{3,2,1,0:T(8,128)} %broadcast.342.clone.2, s32[8]{0:T(128)S(1)} %get-tuple-element.357, f32[8,5,128,128]{3,2,1,0:T(8,128)S(1)} %copy.232), kind=kCustom, calls=%fused_computation.28 | custom fusion | bytes 7864352 | tf_op jit(solution)/shard_map/scatter | solution.py:121
  25.6 51.5 %collective-permute-done = f32[2,4,5,128,128]{4,3,2,1,0:T(8,128)} collective-permute-done((f32[2,4,5,128,128]{4,3,2,1,0:T(8,128)}, f32[2,4,5,128,128]{4,3,2,1,0:T(8,128)}, u32[]{:S(2)}, u32[]{:S(2)}) %collective-permute-start) | collective-permute-done | bytes 2621472 | tf_op jit(solution)/shard_map/ppermute | solution.py:28
  77.1 3.1 %fusion.84 = (f32[1,4,5,128,128]{4,3,2,1,0:T(8,128)}, f32[1,4,5,128,128]{4,3,2,1,0:T(8,128)S(1)}) fusion(f32[2,4,5,128,128]{4,3,2,1,0:T(8,128)} %collective-permute-done), kind=kLoop, calls=%fused_computation.279 | loop fusion | bytes 5242880 | tf_op jit(solution)/shard_map/slice | solution.py:126
  80.2 1.7 pad_maximum_fusion.2
  83.6 3.5 %scatter_fusion = f32[4,5,128,128]{3,2,1,0:T(8,128)} fusion(f32[4,5,128,128]{3,2,1,0:T(8,128)} %broadcast.342.clone.3, s32[8]{0:T(128)S(1)} %get-tuple-element.314, f32[8,5,128,128]{3,2,1,0:T(8,128)S(1)} %copy.232), kind=kCustom, calls=%fused_computation.25 | custom fusion | bytes 7864352 | tf_op jit(solution)/shard_map/scatter | solution.py:121
  87.7 5.5 %pad_maximum_fusion = f32[4,4,5,128,128]{4,3,2,1,0:T(8,128)} fusion(f32[2,4,5,128,128]{4,3,2,1,0:T(8,128)} %collective-permute-done.1, f32[1,4,5,128,128]{4,3,2,1,0:T(8,128)} %get-tuple-element.335, f32[1,4,5,128,128]{4,3,2,1,0:T(8,128)} %bitcast.222), kind=kLoop, calls=%fused_computation.37 | loop fusion | flops 2621440 | bytes 10485760 | tf_op jit(solution)/shard_map/stack | solution.py:126
  93.2 3.1 %gather_fusion = f32[4,5,128,128]{3,2,1,0:T(8,128)S(1)} fusion(f32[4,4,5,128,128]{4,3,2,1,0:T(8,128)} %pad_maximum_fusion, s32[4]{0:T(128)S(1)} %or_reduce_fusion), kind=kCustom, calls=%fused_computation | custom fusion | bytes 2621472 | tf_op jit(solution)/shard_map/gather | solution.py:129
  96.7 2.3 collective-permute-start.3
  99.0 2.1 collective-permute-start.2
  101.1 9.2 %all_gather.12 = f32[32,2,128]{2,1,0:T(2,128)S(1)} all-gather(f32[4,2,128]{2,1,0:T(2,128)S(1)} %pad_maximum_fusion.15), channel_id=1, replica_groups=mesh['blk'=8,'grp'=4] {'blk'}, dimensions={0}, use_global_device_ids=true | all-gather | bytes 36864 | tf_op jit(solution)/shard_map/all_gather | solution.py:75
  114.8 8.1 %while.9 = (s32[]{:T(128)}, f32[4,512]{1,0:T(4,128)S(1)}, s32[4,2]{0,1:T(2,128)S(1)}, f32[4,128]{1,0:T(4,128)S(1)}, s32[]{:T(128)}, /*index=5*/s32[]{:T(128)}) while((s32[]{:T(128)}, f32[4,512]{1,0:T(4,128)S(1)}, s32[4,2]{0,1:T(2,128)S(1)}, f32[4,128]{1,0:T(4,128)S(1)}, s32[]{:T(128)}, /*index=5*/s32[]{:T(128)}) %tuple.234), condition=%wide.while_cond.1, body=%wide.while_body.1.sunk | while | flops 2 | bytes 2161 | solution.py:88
  123.1 8.5 %while.8 = (s32[]{:T(128)}, f32[4,512]{1,0:T(4,128)S(1)}, s32[4,2]{0,1:T(2,128)S(1)}, f32[4,128]{1,0:T(4,128)S(1)}, s32[]{:T(128)}, /*index=5*/s32[]{:T(128)}) while((s32[]{:T(128)}, f32[4,512]{1,0:T(4,128)S(1)}, s32[4,2]{0,1:T(2,128)S(1)}, f32[4,128]{1,0:T(4,128)S(1)}, s32[]{:T(128)}, /*index=5*/s32[]{:T(128)}) %tuple.231), condition=%wide.while_cond, body=%wide.while_body.sunk | while | flops 2 | bytes 2161 | solution.py:85
  123.8 1.4 dynamic-slice.49
  125.9 1.4 dynamic-slice.49
  128.0 1.4 dynamic-slice.49
  130.2 1.4 dynamic-slice.49
  133.4 3.8 %collective-permute-start.4 = (f32[1,4,512]{2,1,0:T(4,128)S(1)}, f32[1,4,512]{2,1,0:T(4,128)S(1)}, u32[]{:S(2)}, u32[]{:S(2)}) collective-permute-start(f32[1,4,512]{2,1,0:T(4,128)S(1)} %maximum_bitcast_fusion.1), channel_id=1, source_target_pairs={{1,0},{2,1},{3,2},{0,3},{5,4},{6,5},{7,6},{4,7},{9,8},{10,9},{11,1... | collective-permute-start | bytes 24584 | tf_op jit(solution)/shard_map/ppermute | solution.py:22
  137.3 9.0 %all_gather.13 = f32[32,2,128]{2,1,0:T(2,128)S(1)} all-gather(f32[4,2,128]{2,1,0:T(2,128)S(1)} %pad_maximum_fusion.16), channel_id=1, replica_groups=mesh['blk'=8,'grp'=4] {'blk'}, dimensions={0}, use_global_device_ids=true | all-gather | bytes 36864 | tf_op jit(solution)/shard_map/all_gather | solution.py:75
  150.7 8.0 %while.11 = (s32[]{:T(128)}, f32[4,512]{1,0:T(4,128)S(1)}, s32[4,2]{0,1:T(2,128)S(1)}, f32[4,128]{1,0:T(4,128)S(1)}, s32[]{:T(128)}, /*index=5*/s32[]{:T(128)}) while((s32[]{:T(128)}, f32[4,512]{1,0:T(4,128)S(1)}, s32[4,2]{0,1:T(2,128)S(1)}, f32[4,128]{1,0:T(4,128)S(1)}, s32[]{:T(128)}, /*index=5*/s32[]{:T(128)}) %tuple.238), condition=%wide.while_cond.3, body=%wide.while_body.3.sunk | while | flops 2 | bytes 2161 | solution.py:88
  151.3 1.4 dynamic-slice.55
  153.3 1.4 dynamic-slice.55
  155.3 1.4 dynamic-slice.55
  157.3 1.4 dynamic-slice.55
  159.0 8.0 %while.10 = (s32[]{:T(128)}, f32[4,512]{1,0:T(4,128)S(1)}, s32[4,2]{0,1:T(2,128)S(1)}, f32[4,128]{1,0:T(4,128)S(1)}, s32[]{:T(128)}, /*index=5*/s32[]{:T(128)}) while((s32[]{:T(128)}, f32[4,512]{1,0:T(4,128)S(1)}, s32[4,2]{0,1:T(2,128)S(1)}, f32[4,128]{1,0:T(4,128)S(1)}, s32[]{:T(128)}, /*index=5*/s32[]{:T(128)}) %tuple.241), condition=%wide.while_cond.2, body=%wide.while_body.2.sunk | while | flops 2 | bytes 2161 | solution.py:85
  159.6 1.4 dynamic-slice.53
  161.6 1.4 dynamic-slice.53
  168.7 3.8 %collective-permute-start.6 = (f32[1,4,512]{2,1,0:T(4,128)S(1)}, f32[1,4,512]{2,1,0:T(4,128)S(1)}, u32[]{:S(2)}, u32[]{:S(2)}) collective-permute-start(f32[1,4,512]{2,1,0:T(4,128)S(1)} %maximum_bitcast_fusion.2), channel_id=1, source_target_pairs={{1,0},{2,1},{3,2},{0,3},{5,4},{6,5},{7,6},{4,7},{9,8},{10,9},{11,1... | collective-permute-start | bytes 24584 | tf_op jit(solution)/shard_map/ppermute | solution.py:22
  172.6 8.3 %all_gather.14 = f32[32,2,128]{2,1,0:T(2,128)S(1)} all-gather(f32[4,2,128]{2,1,0:T(2,128)S(1)} %pad_maximum_fusion.18), channel_id=1, replica_groups=mesh['blk'=8,'grp'=4] {'blk'}, dimensions={0}, use_global_device_ids=true | all-gather | bytes 36864 | tf_op jit(solution)/shard_map/all_gather | solution.py:75
  185.4 8.0 %while.13 = (s32[]{:T(128)}, f32[4,512]{1,0:T(4,128)S(1)}, s32[4,2]{0,1:T(2,128)S(1)}, f32[4,128]{1,0:T(4,128)S(1)}, s32[]{:T(128)}, /*index=5*/s32[]{:T(128)}) while((s32[]{:T(128)}, f32[4,512]{1,0:T(4,128)S(1)}, s32[4,2]{0,1:T(2,128)S(1)}, f32[4,128]{1,0:T(4,128)S(1)}, s32[]{:T(128)}, /*index=5*/s32[]{:T(128)}) %tuple.239), condition=%wide.while_cond.5, body=%wide.while_body.5.sunk | while | flops 2 | bytes 2161 | solution.py:88
  193.7 8.0 %while.12 = (s32[]{:T(128)}, f32[4,512]{1,0:T(4,128)S(1)}, s32[4,2]{0,1:T(2,128)S(1)}, f32[4,128]{1,0:T(4,128)S(1)}, s32[]{:T(128)}, /*index=5*/s32[]{:T(128)}) while((s32[]{:T(128)}, f32[4,512]{1,0:T(4,128)S(1)}, s32[4,2]{0,1:T(2,128)S(1)}, f32[4,128]{1,0:T(4,128)S(1)}, s32[]{:T(128)}, /*index=5*/s32[]{:T(128)}) %tuple.242), condition=%wide.while_cond.4, body=%wide.while_body.4.sunk | while | flops 2 | bytes 2161 | solution.py:85
  203.0 9.0 %all_gather.15 = f32[32,2,128]{2,1,0:T(2,128)S(1)} all-gather(f32[4,2,128]{2,1,0:T(2,128)S(1)} %pad_maximum_fusion.19), channel_id=1, replica_groups=mesh['blk'=8,'grp'=4] {'blk'}, dimensions={0}, use_global_device_ids=true | all-gather | bytes 36864 | tf_op jit(solution)/shard_map/all_gather | solution.py:75
  213.6 3.8 %collective-permute-start.8 = (f32[1,4,512]{2,1,0:T(4,128)S(1)}, f32[1,4,512]{2,1,0:T(4,128)S(1)}, u32[]{:S(2)}, u32[]{:S(2)}) collective-permute-start(f32[1,4,512]{2,1,0:T(4,128)S(1)} %maximum_bitcast_fusion.3), channel_id=1, source_target_pairs={{1,0},{2,1},{3,2},{0,3},{5,4},{6,5},{7,6},{4,7},{9,8},{10,9},{11,1... | collective-permute-start | bytes 24584 | tf_op jit(solution)/shard_map/ppermute | solution.py:22
  217.4 1.6 collective-permute-done.9
  222.2 8.5 %while.14 = (s32[]{:T(128)}, f32[4,512]{1,0:T(4,128)S(1)}, s32[4,2]{0,1:T(2,128)S(1)}, f32[4,128]{1,0:T(4,128)S(1)}, s32[]{:T(128)}, /*index=5*/s32[]{:T(128)}) while((s32[]{:T(128)}, f32[4,512]{1,0:T(4,128)S(1)}, s32[4,2]{0,1:T(2,128)S(1)}, f32[4,128]{1,0:T(4,128)S(1)}, s32[]{:T(128)}, /*index=5*/s32[]{:T(128)}) %tuple.243), condition=%wide.while_cond.6, body=%wide.while_body.6.sunk | while | flops 2 | bytes 2161 | solution.py:85
  222.9 1.4 dynamic-slice.61
  225.0 1.4 dynamic-slice.61
  227.1 1.4 dynamic-slice.61
  229.2 1.4 dynamic-slice.61
  230.8 8.5 %while.15 = (s32[]{:T(128)}, f32[4,512]{1,0:T(4,128)S(1)}, s32[4,2]{0,1:T(2,128)S(1)}, f32[4,128]{1,0:T(4,128)S(1)}, s32[]{:T(128)}, /*index=5*/s32[]{:T(128)}) while((s32[]{:T(128)}, f32[4,512]{1,0:T(4,128)S(1)}, s32[4,2]{0,1:T(2,128)S(1)}, f32[4,128]{1,0:T(4,128)S(1)}, s32[]{:T(128)}, /*index=5*/s32[]{:T(128)}) %tuple.240), condition=%wide.while_cond.7, body=%wide.while_body.7.sunk | while | flops 2 | bytes 2161 | solution.py:88
  231.5 1.4 dynamic-slice.63
  233.6 1.4 dynamic-slice.63
  235.8 1.4 dynamic-slice.63
  237.9 1.4 dynamic-slice.63
  (278 shorter events, 74.5 us)
Async XLA Ops:
  0.6 1.7 copy-start.1
  0.6 1.8 copy-start.2
  2.5 1.0 copy-start.4
  2.5 1.2 copy-start.5
  3.7 0.7 copy-start.7
  16.9 60.2 %collective-permute-start = (f32[2,4,5,128,128]{4,3,2,1,0:T(8,128)}, f32[2,4,5,128,128]{4,3,2,1,0:T(8,128)}, u32[]{:S(2)}, u32[]{:S(2)}) collective-permute-start(f32[2,4,5,128,128]{4,3,2,1,0:T(8,128)} %pad_maximum_fusion.1), channel_id=1, source_target_pairs={{0,8},{4,12},{8,0},{12,4},{16,24},{20,28},{24,16},{28,20},{1,9},{5... | collective-permute-start | bytes 7864328 | tf_op jit(solution)/shard_map/ppermute | solution.py:28
  25.6 54.6 %copy-start = (f32[4,5,128,128]{3,2,1,0:T(8,128)S(1)}, f32[4,5,128,128]{3,2,1,0:T(8,128)}, u32[]{:S(2)}) copy-start(f32[4,5,128,128]{3,2,1,0:T(8,128)} %scatter_fusion.3) | copy-start | bytes 3932164
  80.2 1.7 copy-start.8
  80.2 1.8 copy-start.6
  81.9 5.9 %collective-permute-start.1 = (f32[2,4,5,128,128]{4,3,2,1,0:T(8,128)}, f32[2,4,5,128,128]{4,3,2,1,0:T(8,128)}, u32[]{:S(2)}, u32[]{:S(2)}) collective-permute-start(f32[2,4,5,128,128]{4,3,2,1,0:T(8,128)} %pad_maximum_fusion.2), channel_id=1, source_target_pairs={{0,4},{4,0},{8,12},{12,8},{16,20},{20,16},{24,28},{28,24},{1,5},{5... | collective-permute-start | bytes 7864328 | tf_op jit(solution)/shard_map/ppermute | solution.py:28
  96.7 14.9 %collective-permute-start.3 = (f32[1,4,512]{2,1,0:T(4,128)S(1)}, f32[1,4,512]{2,1,0:T(4,128)S(1)}, u32[]{:S(2)}, u32[]{:S(2)}) collective-permute-start(f32[1,4,512]{2,1,0:T(4,128)S(1)} %maximum_bitcast_fusion), channel_id=1, source_target_pairs={{0,1},{1,2},{2,3},{3,0},{4,5},{5,6},{6,7},{7,4},{8,9},{9,10},{10,1... | collective-permute-start | bytes 24584 | tf_op jit(solution)/shard_map/ppermute | solution.py:21
  99.0 13.4 %collective-permute-start.2 = (f32[1,4,512]{2,1,0:T(4,128)S(1)}, f32[1,4,512]{2,1,0:T(4,128)S(1)}, u32[]{:S(2)}, u32[]{:S(2)}) collective-permute-start(f32[1,4,512]{2,1,0:T(4,128)S(1)} %maximum_bitcast_fusion), channel_id=1, source_target_pairs={{1,0},{2,1},{3,2},{0,3},{5,4},{6,5},{7,6},{4,7},{9,8},{10,9},{11,1... | collective-permute-start | bytes 24584 | tf_op jit(solution)/shard_map/ppermute | solution.py:22
  133.4 14.1 %collective-permute-start.5 = (f32[1,4,512]{2,1,0:T(4,128)S(1)}, f32[1,4,512]{2,1,0:T(4,128)S(1)}, u32[]{:S(2)}, u32[]{:S(2)}) collective-permute-start(f32[1,4,512]{2,1,0:T(4,128)S(1)} %maximum_bitcast_fusion.1), channel_id=1, source_target_pairs={{0,1},{1,2},{2,3},{3,0},{4,5},{5,6},{6,7},{7,4},{8,9},{9,10},{10,1... | collective-permute-start | bytes 24584 | tf_op jit(solution)/shard_map/ppermute | solution.py:21
  133.4 15.4 %collective-permute-start.4 = (f32[1,4,512]{2,1,0:T(4,128)S(1)}, f32[1,4,512]{2,1,0:T(4,128)S(1)}, u32[]{:S(2)}, u32[]{:S(2)}) collective-permute-start(f32[1,4,512]{2,1,0:T(4,128)S(1)} %maximum_bitcast_fusion.1), channel_id=1, source_target_pairs={{1,0},{2,1},{3,2},{0,3},{5,4},{6,5},{7,6},{4,7},{9,8},{10,9},{11,1... | collective-permute-start | bytes 24584 | tf_op jit(solution)/shard_map/ppermute | solution.py:22
  168.7 13.5 %collective-permute-start.7 = (f32[1,4,512]{2,1,0:T(4,128)S(1)}, f32[1,4,512]{2,1,0:T(4,128)S(1)}, u32[]{:S(2)}, u32[]{:S(2)}) collective-permute-start(f32[1,4,512]{2,1,0:T(4,128)S(1)} %maximum_bitcast_fusion.2), channel_id=1, source_target_pairs={{0,1},{1,2},{2,3},{3,0},{4,5},{5,6},{6,7},{7,4},{8,9},{9,10},{10,1... | collective-permute-start | bytes 24584 | tf_op jit(solution)/shard_map/ppermute | solution.py:21
  168.7 14.7 %collective-permute-start.6 = (f32[1,4,512]{2,1,0:T(4,128)S(1)}, f32[1,4,512]{2,1,0:T(4,128)S(1)}, u32[]{:S(2)}, u32[]{:S(2)}) collective-permute-start(f32[1,4,512]{2,1,0:T(4,128)S(1)} %maximum_bitcast_fusion.2), channel_id=1, source_target_pairs={{1,0},{2,1},{3,2},{0,3},{5,4},{6,5},{7,6},{4,7},{9,8},{10,9},{11,1... | collective-permute-start | bytes 24584 | tf_op jit(solution)/shard_map/ppermute | solution.py:22
  203.0 37.1 %copy-start.3 = (f32[4,128,128]{2,1,0:T(8,128)}, f32[4,128,128]{2,1,0:T(8,128)S(1)}, u32[]{:S(2)}) copy-start(f32[4,128,128]{2,1,0:T(8,128)S(1)} %fusion.14) | copy-start | bytes 786436
  213.5 5.5 %collective-permute-start.9 = (f32[1,4,512]{2,1,0:T(4,128)S(1)}, f32[1,4,512]{2,1,0:T(4,128)S(1)}, u32[]{:S(2)}, u32[]{:S(2)}) collective-permute-start(f32[1,4,512]{2,1,0:T(4,128)S(1)} %maximum_bitcast_fusion.3), channel_id=1, source_target_pairs={{0,1},{1,2},{2,3},{3,0},{4,5},{5,6},{6,7},{7,4},{8,9},{9,10},{10,1... | collective-permute-start | bytes 24584 | tf_op jit(solution)/shard_map/ppermute | solution.py:21
  213.6 6.7 %collective-permute-start.8 = (f32[1,4,512]{2,1,0:T(4,128)S(1)}, f32[1,4,512]{2,1,0:T(4,128)S(1)}, u32[]{:S(2)}, u32[]{:S(2)}) collective-permute-start(f32[1,4,512]{2,1,0:T(4,128)S(1)} %maximum_bitcast_fusion.3), channel_id=1, source_target_pairs={{1,0},{2,1},{3,2},{0,3},{5,4},{6,5},{7,6},{4,7},{9,8},{10,9},{11,1... | collective-permute-start | bytes 24584 | tf_op jit(solution)/shard_map/ppermute | solution.py:22
where the time goes:
time: 242 us; the launch traced here: 241 us
  local copies, waits for them, and re-layouts  111 us (46%)
  waiting for transfers between devices  53.1 us (22%)
  blocking collectives  35.5 us (15%)
  other arithmetic  20.7 us (9%)
  starting transfers between devices  19.6 us (8%)
    gather x128, local copies, waits for them, and re-layouts  65.4 us
    ppermute x2, waiting for transfers between devices, partner_2(): lax.ppermute(shard, axis, [(i, i ^ 1 << apart) for i in range(lax.axis_si...  51.5 us
    all_gather x4, blocking collectives, apply_operator(): band_rows = lax.all_gather(top_bottom, 'blk', axis=0, tiled=True)  35.5 us
    scatter x4, local copies, waits for them, and re-layouts, place(): jnp.zeros((blocks,) + fields.shape[1:], jnp.float32).at[index]  13.8 us
    ppermute x4, starting transfers between devices, extended(): after = lax.ppermute(first, axis, down)  13.5 us
    another operation x1, other arithmetic, move_blocks(): arrivals = jnp.stack((place(0), sectioned[0], paired[0], paired[1]))  5.46 us
    another operation x4, local copies, waits for them, and re-layouts  4.91 us
  transfers between devices with their start and end apart: 10, of which 2 were waited for; matrix products, arithmetic and copies ran while one was open for 8% of the time, Pallas kernels for 0%

commit v1 on v0

v1 whole, which is shorter than its diff:
```python
import functools

import jax
import jax.numpy as jnp
from jax import lax
from jax.experimental import pallas as pl
from jax.experimental.pallas import tpu as pltpu
from jax.sharding import PartitionSpec as P

SWEEPS = 4
TAU_MASS = 6.0
LOW_BOUND = 0.2
HIGH_BOUND = 1.9
CHUNK = 32
PAD = 8
MESH = pl.DeviceIdType.MESH
EXACT = lax.Precision.HIGHEST


def relax_weights():
    alpha = 2.0 / (HIGH_BOUND - LOW_BOUND)
    beta = (HIGH_BOUND + LOW_BOUND) / (HIGH_BOUND - LOW_BOUND)
    gamma = beta / alpha
    weight = 2.0 / gamma
    weights = []
    for _ in range(SWEEPS - 1):
        weight = 1.0 / (gamma - weight / (4.0 * alpha**2))
        weights.append((weight, gamma * weight - 1.0))
    return gamma, weights


def kernel(
    owners,
    bands,
    depth_hbm,
    dx_hbm,
    dy_hbm,
    forcing_hbm,
    mask_hbm,
    dest_smem,
    dest_row,
    neigh,
    sol_out,
    res_out,
    depth_v,
    dx_v,
    dy_v,
    forcing_v,
    mask_v,
    coef_x,
    coef_y,
    coef_d,
    inv_d,
    source,
    update,
    field,
    resid,
    table,
    band_tables,
    side_tables,
    pick_rows,
    pick_cols,
    edge_rows,
    edge_cols,
    band_rows,
    side_cols,
    col_tile,
    turned,
    halo_cols,
    find,
    have,
    half_out,
    half_in,
    pair_out,
    pair_in,
    cross_out,
    cross_in,
    load_sems,
    row_send,
    row_recv,
    col_send,
    col_recv,
    move_send,
    move_recv,
):
    slots, height, width = depth_v.shape
    blocks = neigh.shape[0]
    me = lax.axis_index("blk")
    band = lax.axis_index("grp")
    core = me % 2
    sibling = me + 1 - 2 * core
    base = me - me % 4
    inner = me % 4
    east_band = (band + 1) % bands
    west_band = (band + bands - 1) % bands
    half = height // 2

    loads = [
        pltpu.make_async_copy(src, dst, load_sems.at[i])
        for i, (src, dst) in enumerate(
            (
                (dx_hbm, dx_v),
                (dy_hbm, dy_v),
                (depth_hbm, depth_v),
                (mask_hbm, mask_v),
                (forcing_hbm, forcing_v),
            )
        )
    ]
    for load in loads:
        load.start()

    barrier = pltpu.get_barrier_semaphore()
    for step in range(1, owners):
        pl.semaphore_signal(
            barrier, inc=1, device_id=((me + step) % owners, band), device_id_type=MESH
        )
    for step in range(4):
        for side in (east_band, west_band):
            pl.semaphore_signal(
                barrier,
                inc=1,
                device_id=(base + (inner + step) % 4, side),
                device_id_type=MESH,
            )

    table[...] = jnp.zeros_like(table)
    table[0:blocks, 0:8] = (neigh[...] + 1).astype(jnp.float32)
    table[blocks : blocks + 1, 0:slots] = (dest_row[...] + 1).astype(jnp.float32)
    band_tables[0] = table[...]

    targets = (me, sibling, (base + (inner + 2) % 4), (base + (sibling % 4 + 2) % 4))
    for t, target in enumerate(targets):
        for j in range(blocks):
            wanted = (target * bands + band) * blocks + j
            place = jnp.int32(0)
            count = jnp.int32(0)
            for s in range(slots):
                hit = dest_smem[s] == wanted
                place = jnp.where(hit, s, place)
                count = jnp.where(hit, 1, count)
            find[t * blocks + j] = place
            have[t * blocks + j] = count.astype(jnp.float32)

    gamma, weights = relax_weights()
    lane = lax.broadcasted_iota(jnp.int32, (CHUNK, width), 1)
    first_lane = lane == 0
    last_lane = lane == width - 1
    pair = lane // 2

    def put_columns(s, r0, value):
        moved = pltpu.roll(value, 2 * s + 1, 1)
        rows = pl.ds(r0, CHUNK)
        col_tile[rows, :] = jnp.where(pair == s, moved, col_tile[rows, :])

    col_tile[...] = jnp.zeros_like(col_tile)
    for load in loads:
        load.wait()

    def prepare(s, carry):
        for r0 in range(0, height, CHUNK):
            rows = pl.ds(r0, CHUNK)
            ocean = mask_v[s, rows, :].astype(jnp.float32)
            dx = dx_v[s, rows, :]
            dy = dy_v[s, rows, :]
            area = dx * dy
            scaled = depth_v[s, rows, :] * ocean / area
            cx = scaled * (dy * dy)
            cy = scaled * (dx * dx)
            cd = 2.5 * (cx + cy) + TAU_MASS * area
            inv = 1.0 / cd
            src = forcing_v[s, rows, :] * ocean
            start = src * (inv * (1.0 / gamma))
            coef_x[s, rows, :] = cx
            coef_y[s, rows, :] = cy
            coef_d[s, rows, :] = cd
            inv_d[s, rows, :] = inv
            source[s, rows, :] = src
            update[s, rows, :] = start
            field[0, s, pl.ds(PAD + r0, CHUNK), :] = start
            put_columns(s, r0, start)
        return carry

    lax.fori_loop(0, slots, prepare, 0)

    def send_tables():
        for step in range(1, owners):
            pltpu.make_async_remote_copy(
                src_ref=table,
                dst_ref=band_tables.at[owners - step],
                send_sem=row_send.at[SWEEPS],
                recv_sem=row_recv.at[SWEEPS],
                device_id=((me + step) % owners, band),
                device_id_type=MESH,
            ).start()
        for step in range(4):
            for slot, side in ((step, west_band), (4 + step, east_band)):
                pltpu.make_async_remote_copy(
                    src_ref=table,
                    dst_ref=side_tables.at[slot],
                    send_sem=col_send.at[SWEEPS],
                    recv_sem=col_recv.at[SWEEPS],
                    device_id=(base + (inner + step) % 4, side),
                    device_id_type=MESH,
                ).start()

    def send_edges(k):
        now = k % 2
        for s in range(slots):
            edge_rows[k, s : s + 1, :] = field[now, s, PAD : PAD + 1, :]
            edge_rows[k, slots + s : slots + s + 1, :] = field[
                now, s, PAD + height - 1 : PAD + height, :
            ]
        for step in range(1, owners):
            pltpu.make_async_remote_copy(
                src_ref=edge_rows.at[k],
                dst_ref=band_rows.at[k, owners - step],
                send_sem=row_send.at[k],
                recv_sem=row_recv.at[k],
                device_id=((me + step) % owners, band),
                device_id_type=MESH,
            ).start()
        turned[...] = col_tile[...].T
        edge_cols[k, 0] = turned[pl.ds(1, slots, stride=2), :]
        edge_cols[k, 1] = turned[pl.ds(0, slots, stride=2), :]
        for step in range(4):
            for slot, part, side in ((step, 0, west_band), (4 + step, 1, east_band)):
                pltpu.make_async_remote_copy(
                    src_ref=edge_cols.at[k, part],
                    dst_ref=side_cols.at[k, slot],
                    send_sem=col_send.at[k],
                    recv_sem=col_recv.at[k],
                    device_id=(base + (inner + step) % 4, side),
                    device_id_type=MESH,
                ).start()
        band_rows[k, 0] = edge_rows[k]

    def take(ref, sem):
        pltpu.make_async_copy(ref, ref, sem).wait()

    def build_picks():
        take(band_tables.at[pl.ds(1, owners - 1)], row_recv.at[SWEEPS])
        take(side_tables, col_recv.at[SWEEPS])
        lanes = lax.broadcasted_iota(jnp.int32, (2 * slots, width), 1)
        rows = lax.broadcasted_iota(jnp.int32, (2 * slots, width), 0)
        odd = rows % 2 == 1
        mine = jnp.broadcast_to(table[blocks : blocks + 1, :], (2 * slots, width))
        own = jnp.sum(jnp.where(lanes == rows // 2, mine, 0.0), axis=1, keepdims=True)
        group_ids = ((base + lanes // 8) * bands + band) * blocks + lanes % 8 + 1
        known = (lanes % 8 < blocks) & (lanes < 32)
        match = jnp.where(known & (own == group_ids.astype(jnp.float32)), 1.0, 0.0)
        listed = jnp.concatenate(
            [band_tables[(base + g - me + owners) % owners] for g in range(4)], axis=0
        )
        need = jnp.dot(
            match[:, :32], listed, precision=EXACT, preferred_element_type=jnp.float32
        )
        low = lax.broadcasted_iota(jnp.int32, (8, width), 1) < slots
        per_tile = width // (2 * slots)
        wanted = jnp.where(odd, need[:, 1:2], need[:, 0:1])
        for q in range(owners // per_tile):
            ids = jnp.zeros((8, width), jnp.float32)
            for d in range(per_tile):
                tile = jnp.where(low, band_tables[q * per_tile + d], 0.0)
                twice = tile + pltpu.roll(tile, slots, 1)
                ids = ids + (pltpu.roll(twice, 2 * slots * d, 1) if d else twice)
            id_row = jnp.broadcast_to(ids[blocks : blocks + 1, :], (2 * slots, width))
            bottom = (lanes % (2 * slots)) // slots == 1
            good = (wanted == id_row) & (id_row > 0.0) & (bottom != odd)
            pick_rows[:, q * width : (q + 1) * width] = jnp.where(good, 1.0, 0.0)
        ids = jnp.zeros((8, width), jnp.float32)
        for d in range(8):
            tile = jnp.where(low, side_tables[d], 0.0)
            ids = ids + (pltpu.roll(tile, slots * d, 1) if d else tile)
        id_row = jnp.broadcast_to(ids[blocks : blocks + 1, :], (2 * slots, width))
        western = lanes >= 4 * slots
        for i, (east_of, west_of) in enumerate(((2, 3), (4, 5), (6, 7))):
            wanted = jnp.where(
                odd, need[:, west_of : west_of + 1], need[:, east_of : east_of + 1]
            )
            good = (wanted == id_row) & (id_row > 0.0) & (western == odd)
            pick_cols[2 * slots * i : 2 * slots * (i + 1), :] = jnp.where(good, 1.0, 0.0)

    def take_edges(k):
        now = k % 2
        take(band_rows.at[k, pl.ds(1, owners - 1)], row_recv.at[k])
        per_tile = width // (2 * slots)
        got = jnp.zeros((2 * slots, width), jnp.float32)
        for q in range(owners // per_tile):
            got = got + jnp.dot(
                pick_rows[:, q * width : (q + 1) * width],
                band_rows[k, q * per_tile : (q + 1) * per_tile].reshape(width, width),
                precision=EXACT,
                preferred_element_type=jnp.float32,
            )
        for s in range(slots):
            field[now, s, PAD - 1 : PAD, :] = got[2 * s : 2 * s + 1, :]
            field[now, s, PAD + height : PAD + height + 1, :] = got[2 * s + 1 : 2 * s + 2, :]
        take(side_cols.at[k], col_recv.at[k])
        count = 8 * slots
        cols = jnp.dot(
            pick_cols[:, 0:count],
            side_cols[k].reshape(count, width),
            precision=EXACT,
            preferred_element_type=jnp.float32,
        )
        lanes = lax.broadcasted_iota(jnp.int32, (2 * slots, width), 1)
        straight = cols[0 : 2 * slots]
        above = jnp.where(lanes == width - 1, cols[2 * slots : 4 * slots], straight)
        below = jnp.where(lanes == 0, cols[4 * slots : 6 * slots], straight)
        slanted = pltpu.roll(above, 1, 1) + pltpu.roll(below, width - 1, 1)
        filled = jnp.concatenate(
            [straight, slanted, jnp.zeros((width - 4 * slots, width), jnp.float32)], axis=0
        )
        halo_cols[...] = filled.T

    def around(value, halo):
        left = jnp.where(first_lane, halo, pltpu.roll(value, 1, 1))
        right = jnp.where(last_lane, halo, pltpu.roll(value, width - 1, 1))
        return left + right

    def sweep(k):
        now = k % 2

        def one(s, carry):
            for r0 in range(0, height, CHUNK):
                rows = pl.ds(r0, CHUNK)
                center = field[now, s, pl.ds(PAD + r0, CHUNK), :]
                north = field[now, s, pl.ds(PAD + r0 - 1, CHUNK), :]
                south = field[now, s, pl.ds(PAD + r0 + 1, CHUNK), :]
                vertical = north + south
                cols = halo_cols[rows, :]
                level = around(center, pltpu.roll(cols, width - 1 - 2 * s, 1))
                slant = around(vertical, pltpu.roll(cols, width - 1 - 2 * slots - 2 * s, 1))
                slant = 0.125 * slant
                left = (
                    source[s, rows, :]
                    - coef_d[s, rows, :] * center
                    + coef_x[s, rows, :] * (level + slant)
                    + coef_y[s, rows, :] * (vertical + slant)
                )
                if k == SWEEPS - 1:
                    resid[s, rows, :] = left
                else:
                    weight, keep = weights[k]
                    change = weight * left * inv_d[s, rows, :] + keep * update[s, rows, :]
                    update[s, rows, :] = change
                    fresh = center + change
                    field[1 - now, s, pl.ds(PAD + r0, CHUNK), :] = fresh
                    put_columns(s, r0, fresh)
            return carry

        lax.fori_loop(0, slots, one, 0)

    last = (SWEEPS - 1) % 2

    def rows_of(f, slot, r0, count):
        if f == 0:
            return field[last, slot, pl.ds(PAD + r0, count), :]
        return resid[slot, pl.ds(r0, count), :]

    def start_move(f):
        away = (1 - core) * half

        def fill_half(i, carry):
            slot = find[2 * blocks + i]
            half_out[f, i] = rows_of(f, slot, away, half) * have[2 * blocks + i]
            return carry

        lax.fori_loop(0, 2 * blocks, fill_half, 0)
        pltpu.make_async_remote_copy(
            src_ref=half_out.at[f],
            dst_ref=half_in.at[f],
            send_sem=move_send.at[f, 0],
            recv_sem=move_recv.at[f, 0],
            device_id=(sibling, band),
            device_id_type=MESH,
        ).start()

        def fill_pair(i, carry):
            slot = find[blocks + i]
            pair_out[f, i] = rows_of(f, slot, 0, height) * have[blocks + i]
            return carry

        lax.fori_loop(0, blocks, fill_pair, 0)
        pltpu.make_async_remote_copy(
            src_ref=pair_out.at[f],
            dst_ref=pair_in.at[f],
            send_sem=move_send.at[f, 1],
            recv_sem=move_recv.at[f, 1],
            device_id=(sibling, band),
            device_id_type=MESH,
        ).start()

    def cross_move(f):
        kept = core * half
        take(half_in.at[f], move_recv.at[f, 0])
        for t in range(2):

            def fill(i, carry, t=t):
                slot = find[(2 + t) * blocks + i]
                cross_out[f, t, i] = (
                    rows_of(f, slot, kept, half) * have[(2 + t) * blocks + i]
                    + half_in[f, (1 - t) * blocks + i]
                )
                return carry

            lax.fori_loop(0, blocks, fill, 0)
            pltpu.make_async_remote_copy(
                src_ref=cross_out.at[f, t],
                dst_ref=cross_in.at[f, core],
                send_sem=move_send.at[f, 2 + t],
                recv_sem=move_recv.at[f, 2],
                device_id=(targets[2 + t], band),
                device_id_type=MESH,
            ).start()

    def finish_move(f, out):
        take(pair_in.at[f], move_recv.at[f, 1])

        def near(i, carry):
            out[i] = rows_of(f, find[i], 0, height) * have[i] + pair_in[f, i]
            return carry

        lax.fori_loop(0, blocks, near, 0)
        take(cross_in.at[f], move_recv.at[f, 2])

        def far(i, carry):
            for h in range(2):
                rows = pl.ds(h * half, half)
                out[i, rows, :] = out[i, rows, :] + cross_in[f, h, i]
            return carry

        lax.fori_loop(0, blocks, far, 0)

    pl.semaphore_wait(barrier, owners - 1 + 8)
    send_tables()
    send_edges(0)
    build_picks()
    for k in range(SWEEPS):
        if k == SWEEPS - 1:
            start_move(0)
            cross_move(0)
        take_edges(k)
        sweep(k)
        if k < SWEEPS - 1:
            send_edges(k + 1)
    start_move(1)
    cross_move(1)
    finish_move(0, sol_out)
    finish_move(1, res_out)

    take(band_tables.at[pl.ds(1, owners - 1)], row_send.at[SWEEPS])
    take(side_tables, col_send.at[SWEEPS])
    for k in range(SWEEPS):
        take(band_rows.at[k, pl.ds(1, owners - 1)], row_send.at[k])
        take(side_cols.at[k], col_send.at[k])
    for f in range(2):
        take(half_out.at[f], move_send.at[f, 0])
        take(pair_out.at[f], move_send.at[f, 1])
        take(cross_out.at[f, 0], move_send.at[f, 2])
        take(cross_out.at[f, 1], move_send.at[f, 3])


def per_device(
    owners, bands, depth, cell_dx, cell_dy, forcing, land_mask, dest_block, source_slot, neighbours
):
    slots, height, width = depth.shape
    blocks = source_slot.shape[0]
    half = height // 2
    f32 = jnp.float32
    any_spec = pl.BlockSpec(memory_space=pl.ANY)
    vmem = pl.BlockSpec(memory_space=pltpu.VMEM)
    whole = pltpu.VMEM((slots, height, width), f32)
    dma = pltpu.SemaphoreType.DMA
    out = jax.ShapeDtypeStruct((blocks, height, width), f32)
    return pl.pallas_call(
        functools.partial(kernel, owners, bands),
        out_shape=(out, out),
        in_specs=[any_spec] * 5 + [pl.BlockSpec(memory_space=pltpu.SMEM), vmem, vmem],
        out_specs=(vmem, vmem),
        scratch_shapes=[
            whole,
            whole,
            whole,
            whole,
            pltpu.VMEM((slots, height, width), jnp.int32),
            whole,
            whole,
            whole,
            whole,
            whole,
            whole,
            pltpu.VMEM((2, slots, height + 2 * PAD, width), f32),
            whole,
            pltpu.VMEM((8, width), f32),
            pltpu.VMEM((owners, 8, width), f32),
            pltpu.VMEM((8, 8, width), f32),
            pltpu.VMEM((2 * slots, owners * 2 * slots), f32),
            pltpu.VMEM((6 * slots, width), f32),
            pltpu.VMEM((SWEEPS, 2 * slots, width), f32),
            pltpu.VMEM((SWEEPS, 2, slots, width), f32),
            pltpu.VMEM((SWEEPS, owners, 2 * slots, width), f32),
            pltpu.VMEM((SWEEPS, 8, slots, width), f32),
            pltpu.VMEM((height, width), f32),
            pltpu.VMEM((width, height), f32),
            pltpu.VMEM((height, width), f32),
            pltpu.SMEM((4 * blocks,), jnp.int32),
            pltpu.SMEM((4 * blocks,), f32),
            pltpu.VMEM((2, 2 * blocks, half, width), f32),
            pltpu.VMEM((2, 2 * blocks, half, width), f32),
            pltpu.VMEM((2, blocks, height, width), f32),
            pltpu.VMEM((2, blocks, height, width), f32),
            pltpu.VMEM((2, 2, blocks, half, width), f32),
            pltpu.VMEM((2, 2, blocks, half, width), f32),
            dma((5,)),
            dma((SWEEPS + 1,)),
            dma((SWEEPS + 1,)),
            dma((SWEEPS + 1,)),
            dma((SWEEPS + 1,)),
            dma((2, 4)),
            dma((2, 3)),
        ],
        compiler_params=pltpu.CompilerParams(
            collective_id=0, has_side_effects=True, vmem_limit_bytes=40 * 1024 * 1024
        ),
        name="barotropic_solve",
    )(
        depth,
        cell_dx,
        cell_dy,
        forcing,
        land_mask,
        dest_block,
        dest_block.reshape(1, slots),
        neighbours,
    )


def solution(mesh):
    blocks3 = P(("blk", "grp"), None, None)
    flat = P(("blk", "grp"))
    in_specs = (blocks3,) * 5 + (flat, flat, P(("blk", "grp"), None))
    return jax.shard_map(
        functools.partial(per_device, mesh.shape["blk"], mesh.shape["grp"]),
        mesh=mesh,
        in_specs=in_specs,
        out_specs=(blocks3, blocks3),
        check_vma=False,
    )
```

time: 242 us -> 51.8 us (0.21)
  local copies, waits for them, and re-layouts: 111 us -> 7.94 us
  waiting for transfers between devices: 53.1 us -> 0 us
  Pallas kernels: 0 us -> 42.8 us
  blocking collectives: 35.5 us -> 0 us
  other arithmetic: 20.7 us -> 0 us
  starting transfers between devices: 19.6 us -> 0 us
    gather x177 -> x0, local copies, waits for them, and re-layouts: 86.1 us -> none
    ppermute x10 -> x0, waiting for transfers between devices: 53.1 us -> none  [the longest x2 51.5 us: partner_2(): lax.ppermute(shard, axis, [(i, i ^ 1 << apart) for i in range(lax.axis_si...]
    pallas_call x0 -> x1, Pallas kernels: none -> 42.8 us  [per_device(): pl.pallas_call(functools.partial(kernel, owners, bands), out_shape=(out,...]
    all_gather x4 -> x0, blocking collectives: 35.5 us -> none  [apply_operator(): band_rows = lax.all_gather(top_bottom, 'blk', axis=0, tiled=True)]
    ppermute x10 -> x0, starting transfers between devices: 19.6 us -> none  [the longest x4 13.5 us: extended(): after = lax.ppermute(first, axis, down)]
    scatter x4 -> x0, local copies, waits for them, and re-layouts: 13.8 us -> none  [place(): jnp.zeros((blocks,) + fields.shape[1:], jnp.float32).at[index]]
    another operation x8 -> x0, other arithmetic: 10.8 us -> none  [the longest x1 5.46 us: move_blocks(): arrivals = jnp.stack((place(0), sectioned[0], paired[0], paired[1]))]
    unnamed x28 -> x16, local copies, waits for them, and re-layouts: 1.43 us -> 7.94 us
  transfers between devices with their start and end apart: 10 -> 0, of which waited for: 2 -> 0; matrix products, arithmetic and copies ran while one was open for 8% -> 0% of each run, Pallas kernels for 0% -> 0%
where the time goes in v1:
time: 51.8 us; the launch traced here: 51.4 us
  Pallas kernels  42.8 us (83%)
  local copies, waits for them, and re-layouts  7.94 us (15%)
  between operations  0.66 us (1%)
    pallas_call x1, Pallas kernels, per_device(): pl.pallas_call(functools.partial(kernel, owners, bands), out_shape=(out,...  42.8 us
    unnamed x16, local copies, waits for them, and re-layouts  7.94 us

profile of v1, /device:TPU:0, one launch (start us, length us, event | category | flops | bytes accessed | tf_op | source)
XLA Modules:
  0.0 51.4 jit_solution(2843988603354941214)
XLA Ops:
  0.6 0.0 copy-start.6
  0.6 0.6 %copy-done.6 = s32[8]{0:T(128)S(1)} copy-done((s32[8]{0:T(128)S(1)}, s32[8]{0:T(128)}, u32[]{:S(2)}) %copy-start.6) | copy-done | bytes 56
  1.3 0.0 copy-start
  1.3 1.0 %copy-done = f32[8,128,128]{2,1,0:T(8,128)S(1)} copy-done((f32[8,128,128]{2,1,0:T(8,128)S(1)}, f32[8,128,128]{2,1,0:T(8,128)}, u32[]{:S(2)}) %copy-start) | copy-done | bytes 524312
  2.3 0.0 copy-start.1
  2.3 1.0 %copy-done.1 = f32[8,128,128]{2,1,0:T(8,128)S(1)} copy-done((f32[8,128,128]{2,1,0:T(8,128)S(1)}, f32[8,128,128]{2,1,0:T(8,128)}, u32[]{:S(2)}) %copy-start.1) | copy-done | bytes 524312
  3.4 0.0 copy-start.2
  3.4 1.0 %copy-done.2 = f32[8,128,128]{2,1,0:T(8,128)S(1)} copy-done((f32[8,128,128]{2,1,0:T(8,128)S(1)}, f32[8,128,128]{2,1,0:T(8,128)}, u32[]{:S(2)}) %copy-start.2) | copy-done | bytes 524312
  4.4 0.0 copy-start.3
  4.4 1.0 %copy-done.3 = f32[8,128,128]{2,1,0:T(8,128)S(1)} copy-done((f32[8,128,128]{2,1,0:T(8,128)S(1)}, f32[8,128,128]{2,1,0:T(8,128)}, u32[]{:S(2)}) %copy-start.3) | copy-done | bytes 524312
  5.5 0.0 copy-start.4
  5.5 1.0 %copy-done.4 = s32[8,128,128]{2,1,0:T(8,128)S(1)} copy-done((s32[8,128,128]{2,1,0:T(8,128)S(1)}, s32[8,128,128]{2,1,0:T(8,128)}, u32[]{:S(2)}) %copy-start.4) | copy-done | bytes 524312
  6.5 0.0 copy-start.5
  6.5 0.7 %copy-done.5 = s32[4,8]{1,0:T(4,128)S(1)} copy-done((s32[4,8]{1,0:T(4,128)S(1)}, s32[4,8]{1,0:T(4,128)}, u32[]{:S(2)}) %copy-start.5) | copy-done | bytes 152
  7.2 42.8 %barotropic_solve.1 = (f32[4,128,128]{2,1,0:T(8,128)S(1)}, f32[4,128,128]{2,1,0:T(8,128)S(1)}) custom-call(f32[8,128,128]{2,1,0:T(8,128)S(1)} %copy-done, f32[8,128,128]{2,1,0:T(8,128)S(1)} %copy-done.1, f32[8,128,128]{2,1,0:T(8,128)S(1)} %copy-done.2, f32[8,128,128]{2,1,0:T(8,128)S(1)} %copy-done.3, s32[8,128,128]{2,1,0:T(8,128)S(1)} %copy-done.4, ...), custom_call_target="tpu_custom_call" | custom-call | tf_op jit(solution)/shard_map/barotropic_solve/pallas_call | solution.py:477
  50.0 0.7 %copy.11 = f32[4,128,128]{2,1,0:T(8,128)} copy(f32[4,128,128]{2,1,0:T(8,128)S(1)} %get-tuple-element.4) | data formatting | bytes 524288
  50.7 0.7 %copy.12 = f32[4,128,128]{2,1,0:T(8,128)} copy(f32[4,128,128]{2,1,0:T(8,128)S(1)} %get-tuple-element.5) | data formatting | bytes 524288
Async XLA Ops:
  0.6 0.7 %copy-start.6 = (s32[8]{0:T(128)S(1)}, s32[8]{0:T(128)}, u32[]{:S(2)}) copy-start(s32[8]{0:T(128)} %dest_smem.1) | copy-start | bytes 100
  1.3 1.0 %copy-start = (f32[8,128,128]{2,1,0:T(8,128)S(1)}, f32[8,128,128]{2,1,0:T(8,128)}, u32[]{:S(2)}) copy-start(f32[8,128,128]{2,1,0:T(8,128)} %depth_hbm.1) | copy-start | bytes 1572868
  2.3 1.0 %copy-start.1 = (f32[8,128,128]{2,1,0:T(8,128)S(1)}, f32[8,128,128]{2,1,0:T(8,128)}, u32[]{:S(2)}) copy-start(f32[8,128,128]{2,1,0:T(8,128)} %dx_hbm.1) | copy-start | bytes 1572868
  3.4 1.0 %copy-start.2 = (f32[8,128,128]{2,1,0:T(8,128)S(1)}, f32[8,128,128]{2,1,0:T(8,128)}, u32[]{:S(2)}) copy-start(f32[8,128,128]{2,1,0:T(8,128)} %dy_hbm.1) | copy-start | bytes 1572868
  4.4 1.0 %copy-start.3 = (f32[8,128,128]{2,1,0:T(8,128)S(1)}, f32[8,128,128]{2,1,0:T(8,128)}, u32[]{:S(2)}) copy-start(f32[8,128,128]{2,1,0:T(8,128)} %forcing_hbm.1) | copy-start | bytes 1572868
  5.5 1.0 %copy-start.4 = (s32[8,128,128]{2,1,0:T(8,128)S(1)}, s32[8,128,128]{2,1,0:T(8,128)}, u32[]{:S(2)}) copy-start(s32[8,128,128]{2,1,0:T(8,128)} %mask_hbm.1) | copy-start | bytes 1572868
  6.5 0.7 %copy-start.5 = (s32[4,8]{1,0:T(4,128)S(1)}, s32[4,8]{1,0:T(4,128)}, u32[]{:S(2)}) copy-start(s32[4,8]{1,0:T(4,128)} %neigh.1) | copy-start | bytes 388

commit v2 on v1

--- a/solution.py
+++ b/solution.py
@@ -65,7 +65,10 @@
     band_rows,
     side_cols,
     col_tile,
-    turned,
+    row_coefs,
+    col_coefs,
+    inner_cols,
+    filled,
     halo_cols,
     find,
     have,
@@ -146,12 +149,13 @@
     lane = lax.broadcasted_iota(jnp.int32, (CHUNK, width), 1)
     first_lane = lane == 0
     last_lane = lane == width - 1
-    pair = lane // 2
-
-    def put_columns(s, r0, value):
-        moved = pltpu.roll(value, 2 * s + 1, 1)
+
+    def put_columns(at, s, r0, value, deep):
         rows = pl.ds(r0, CHUNK)
-        col_tile[rows, :] = jnp.where(pair == s, moved, col_tile[rows, :])
+        right = pltpu.roll(value, at + 1 + deep + s, 1)
+        left = pltpu.roll(value, at + slots - deep + s, 1)
+        tile = jnp.where(lane == at + s, right, col_tile[rows, :])
+        col_tile[rows, :] = jnp.where(lane == at + slots + s, left, tile)
 
     col_tile[...] = jnp.zeros_like(col_tile)
     for load in loads:
@@ -178,10 +182,21 @@
             source[s, rows, :] = src
             update[s, rows, :] = start
             field[0, s, pl.ds(PAD + r0, CHUNK), :] = start
-            put_columns(s, r0, start)
+            parts = (cx, cy, cd, inv, src, start, start)
+            for i, part in enumerate(parts):
+                put_columns(2 * slots * i, s, r0, part, 1 if i == 6 else 0)
         return carry
 
     lax.fori_loop(0, slots, prepare, 0)
+    col_coefs[...] = col_tile[...].T
+    inner_cols[...] = col_coefs[12 * slots : 14 * slots, :]
+    filled[...] = jnp.zeros_like(filled)
+    for i, ref in enumerate((coef_x, coef_y, coef_d, inv_d, source, update)):
+        for s in range(slots):
+            row_coefs[i, s : s + 1, :] = ref[s, 0:1, :]
+            row_coefs[i, slots + s : slots + s + 1, :] = ref[s, height - 1 : height, :]
+    edge_rows[0] = row_coefs[5]
+    edge_cols[0] = col_coefs[10 * slots : 12 * slots, :]
 
     def send_tables():
         for step in range(1, owners):
@@ -205,12 +220,6 @@
                 ).start()
 
     def send_edges(k):
-        now = k % 2
-        for s in range(slots):
-            edge_rows[k, s : s + 1, :] = field[now, s, PAD : PAD + 1, :]
-            edge_rows[k, slots + s : slots + s + 1, :] = field[
-                now, s, PAD + height - 1 : PAD + height, :
-            ]
         for step in range(1, owners):
             pltpu.make_async_remote_copy(
                 src_ref=edge_rows.at[k],
@@ -220,13 +229,10 @@
                 device_id=((me + step) % owners, band),
                 device_id_type=MESH,
             ).start()
-        turned[...] = col_tile[...].T
-        edge_cols[k, 0] = turned[pl.ds(1, slots, stride=2), :]
-        edge_cols[k, 1] = turned[pl.ds(0, slots, stride=2), :]
         for step in range(4):
-            for slot, part, side in ((step, 0, west_band), (4 + step, 1, east_band)):
+            for slot, part, side in ((step, slots, west_band), (4 + step, 0, east_band)):
                 pltpu.make_async_remote_copy(
-                    src_ref=edge_cols.at[k, part],
+                    src_ref=edge_cols.at[k, pl.ds(part, slots)],
                     dst_ref=side_cols.at[k, slot],
                     send_sem=col_send.at[k],
                     recv_sem=col_recv.at[k],
@@ -243,9 +249,9 @@
         take(side_tables, col_recv.at[SWEEPS])
         lanes = lax.broadcasted_iota(jnp.int32, (2 * slots, width), 1)
         rows = lax.broadcasted_iota(jnp.int32, (2 * slots, width), 0)
-        odd = rows % 2 == 1
+        lower = rows >= slots
         mine = jnp.broadcast_to(table[blocks : blocks + 1, :], (2 * slots, width))
-        own = jnp.sum(jnp.where(lanes == rows // 2, mine, 0.0), axis=1, keepdims=True)
+        own = jnp.sum(jnp.where(lanes == rows % slots, mine, 0.0), axis=1, keepdims=True)
         group_ids = ((base + lanes // 8) * bands + band) * blocks + lanes % 8 + 1
         known = (lanes % 8 < blocks) & (lanes < 32)
         match = jnp.where(known & (own == group_ids.astype(jnp.float32)), 1.0, 0.0)
@@ -257,7 +263,7 @@
         )
         low = lax.broadcasted_iota(jnp.int32, (8, width), 1) < slots
         per_tile = width // (2 * slots)
-        wanted = jnp.where(odd, need[:, 1:2], need[:, 0:1])
+        wanted = jnp.where(lower, need[:, 1:2], need[:, 0:1])
         for q in range(owners // per_tile):
             ids = jnp.zeros((8, width), jnp.float32)
             for d in range(per_tile):
@@ -266,7 +272,7 @@
                 ids = ids + (pltpu.roll(twice, 2 * slots * d, 1) if d else twice)
             id_row = jnp.broadcast_to(ids[blocks : blocks + 1, :], (2 * slots, width))
             bottom = (lanes % (2 * slots)) // slots == 1
-            good = (wanted == id_row) & (id_row > 0.0) & (bottom != odd)
+            good = (wanted == id_row) & (id_row > 0.0) & (bottom != lower)
             pick_rows[:, q * width : (q + 1) * width] = jnp.where(good, 1.0, 0.0)
         ids = jnp.zeros((8, width), jnp.float32)
         for d in range(8):
@@ -276,9 +282,9 @@
         western = lanes >= 4 * slots
         for i, (east_of, west_of) in enumerate(((2, 3), (4, 5), (6, 7))):
             wanted = jnp.where(
-                odd, need[:, west_of : west_of + 1], need[:, east_of : east_of + 1]
+                lower, need[:, west_of : west_of + 1], need[:, east_of : east_of + 1]
             )
-            good = (wanted == id_row) & (id_row > 0.0) & (western == odd)
+            good = (wanted == id_row) & (id_row > 0.0) & (western == lower)
             pick_cols[2 * slots * i : 2 * slots * (i + 1), :] = jnp.where(good, 1.0, 0.0)
 
     def take_edges(k):
@@ -294,8 +300,8 @@
                 preferred_element_type=jnp.float32,
             )
         for s in range(slots):
-            field[now, s, PAD - 1 : PAD, :] = got[2 * s : 2 * s + 1, :]
-            field[now, s, PAD + height : PAD + height + 1, :] = got[2 * s + 1 : 2 * s + 2, :]
+            field[now, s, PAD - 1 : PAD, :] = got[s : s + 1, :]
+            field[now, s, PAD + height : PAD + height + 1, :] = got[slots + s : slots + s + 1, :]
         take(side_cols.at[k], col_recv.at[k])
         count = 8 * slots
         cols = jnp.dot(
@@ -309,10 +315,63 @@
         above = jnp.where(lanes == width - 1, cols[2 * slots : 4 * slots], straight)
         below = jnp.where(lanes == 0, cols[4 * slots : 6 * slots], straight)
         slanted = pltpu.roll(above, 1, 1) + pltpu.roll(below, width - 1, 1)
-        filled = jnp.concatenate(
-            [straight, slanted, jnp.zeros((width - 4 * slots, width), jnp.float32)], axis=0
+        for i, tile in enumerate((straight, slanted)):
+            for h in range(2):
+                filled[pl.ds(2 * slots * i + h, slots, stride=2), :] = tile[
+                    slots * h : slots * (h + 1)
+                ]
+        return got, straight, slanted
+
+    def stencil(coefs, center, level, vertical, slant):
+        cx, cy, cd, inv, src = (coefs[i] for i in range(5))
+        slant = 0.125 * slant
+        return (src - cd * center + cx * (level + slant) + cy * (vertical + slant)) * inv
+
+    def ring(k, got, straight, slanted):
+        now = k % 2
+        weight, keep = weights[k]
+        lanes = lax.broadcasted_iota(jnp.int32, (2 * slots, width), 1)
+        start = lanes == 0
+        end = lanes == width - 1
+
+        def spread(value, before, after):
+            left = jnp.where(start, before, pltpu.roll(value, 1, 1))
+            return left + jnp.where(end, after, pltpu.roll(value, width - 1, 1))
+
+        def ends(tile, at):
+            part = tile[at : at + slots]
+            return jnp.concatenate([part[:, 0:1], part[:, width - 1 : width]], axis=0)
+
+        center = edge_rows[k]
+        inside = jnp.concatenate(
+            [field[now, s, PAD + 1 : PAD + 2, :] for s in range(slots)]
+            + [field[now, s, PAD + height - 2 : PAD + height - 1, :] for s in range(slots)],
+            axis=0,
         )
-        halo_cols[...] = filled.T
+        vertical = inside + got
+        level = spread(center, ends(straight, slots), ends(straight, 0))
+        slant = spread(vertical, ends(slanted, slots), ends(slanted, 0))
+        left = stencil([row_coefs[i] for i in range(5)], center, level, vertical, slant)
+        change = weight * left + keep * row_coefs[5]
+        row_coefs[5] = change
+        edge_rows[k + 1] = center + change
+
+        def sides(at, deep):
+            part = got[at : at + slots]
+            last = width - 1 - deep
+            return jnp.concatenate([part[:, last : last + 1], part[:, deep : deep + 1]], axis=0)
+
+        center = edge_cols[k]
+        inside = inner_cols[...]
+        level = inside + straight
+        vertical = spread(center, sides(0, 0), sides(slots, 0))
+        slant = slanted + spread(inside, sides(0, 1), sides(slots, 1))
+        tall = 2 * slots
+        coefs = [col_coefs[i * tall : (i + 1) * tall, :] for i in range(5)]
+        left = stencil(coefs, center, level, vertical, slant)
+        change = weight * left + keep * col_coefs[5 * tall : 6 * tall, :]
+        col_coefs[5 * tall : 6 * tall, :] = change
+        edge_cols[k + 1] = center + change
 
     def around(value, halo):
         left = jnp.where(first_lane, halo, pltpu.roll(value, 1, 1))
@@ -347,10 +406,13 @@
                     update[s, rows, :] = change
                     fresh = center + change
                     field[1 - now, s, pl.ds(PAD + r0, CHUNK), :] = fresh
-                    put_columns(s, r0, fresh)
+                    put_columns(0, s, r0, fresh, 1)
             return carry
 
+        halo_cols[...] = filled[...].T
         lax.fori_loop(0, slots, one, 0)
+        if k < SWEEPS - 1:
+            inner_cols[...] = col_tile[...].T[0 : 2 * slots]
 
     last = (SWEEPS - 1) % 2
 
@@ -441,10 +503,11 @@
         if k == SWEEPS - 1:
             start_move(0)
             cross_move(0)
-        take_edges(k)
+        halo = take_edges(k)
+        if k < SWEEPS - 1:
+            ring(k, *halo)
+            send_edges(k + 1)
         sweep(k)
-        if k < SWEEPS - 1:
-            send_edges(k + 1)
     start_move(1)
     cross_move(1)
     finish_move(0, sol_out)
@@ -499,10 +562,13 @@
             pltpu.VMEM((2 * slots, owners * 2 * slots), f32),
             pltpu.VMEM((6 * slots, width), f32),
             pltpu.VMEM((SWEEPS, 2 * slots, width), f32),
-            pltpu.VMEM((SWEEPS, 2, slots, width), f32),
+            pltpu.VMEM((SWEEPS, 2 * slots, width), f32),
             pltpu.VMEM((SWEEPS, owners, 2 * slots, width), f32),
             pltpu.VMEM((SWEEPS, 8, slots, width), f32),
             pltpu.VMEM((height, width), f32),
+            pltpu.VMEM((6, 2 * slots, width), f32),
+            pltpu.VMEM((width, height), f32),
+            pltpu.VMEM((2 * slots, width), f32),
             pltpu.VMEM((width, height), f32),
             pltpu.VMEM((height, width), f32),
             pltpu.SMEM((4 * blocks,), jnp.int32),
@@ -522,7 +588,7 @@
             dma((2, 3)),
         ],
         compiler_params=pltpu.CompilerParams(
-            collective_id=0, has_side_effects=True, vmem_limit_bytes=40 * 1024 * 1024
+            collective_id=0, has_side_effects=True, vmem_limit_bytes=60 * 1024 * 1024
         ),
         name="barotropic_solve",
     )(

time: 51.8 us -> 43.9 us (0.85)
  local copies, waits for them, and re-layouts: 7.94 us -> 2.42 us
  Pallas kernels: 42.8 us -> 40.7 us
    unnamed x16 -> x4, local copies, waits for them, and re-layouts: 7.94 us -> 2.42 us
    pallas_call x1, Pallas kernels: 42.8 us -> 40.7 us  [per_device(): pl.pallas_call(functools.partial(kernel, owners, bands), out_shape=(out,...]
where the time goes in v2:
time: 43.9 us; the launch traced here: 43.7 us
  Pallas kernels  40.7 us (93%)
  local copies, waits for them, and re-layouts  2.42 us (6%)
  between operations  0.65 us (1%)
    pallas_call x1, Pallas kernels, per_device(): pl.pallas_call(functools.partial(kernel, owners, bands), out_shape=(out,...  40.7 us
    unnamed x4, local copies, waits for them, and re-layouts  2.42 us

profile of v2, /device:TPU:0, one launch (start us, length us, event | category | flops | bytes accessed | tf_op | source)
XLA Modules:
  0.0 43.7 jit_solution(2509366492703300008)
XLA Ops:
  0.6 40.7 %barotropic_solve.1 = (f32[4,128,128]{2,1,0:T(8,128)}, f32[4,128,128]{2,1,0:T(8,128)}) custom-call(f32[8,128,128]{2,1,0:T(8,128)} %depth_hbm.1, f32[8,128,128]{2,1,0:T(8,128)} %dx_hbm.1, f32[8,128,128]{2,1,0:T(8,128)} %dy_hbm.1, f32[8,128,128]{2,1,0:T(8,128)} %forcing_hbm.1, s32[8,128,128]{2,1,0:T(8,128)} %mask_hbm.1, s32[8]{0:T(128)} %dest_smem.1, ...), custom_call_target="tpu_custom_call" | custom-call | tf_op jit(solution)/shard_map/barotropic_solve/pallas_call | solution.py:540
  41.3 0.0 copy-start
  41.3 1.7 %copy.11 = f32[4,128,128]{2,1,0:T(8,128)} copy(f32[4,128,128]{2,1,0:T(8,128)} %get-tuple-element.4) | data formatting | bytes 524288
  43.0 0.0 copy-done
  43.0 0.7 %copy.12 = f32[4,128,128]{2,1,0:T(8,128)} copy(f32[4,128,128]{2,1,0:T(8,128)S(1)} %copy-done) | data formatting | bytes 524288
Async XLA Ops:
  41.3 1.7 %copy-start = (f32[4,128,128]{2,1,0:T(8,128)S(1)}, f32[4,128,128]{2,1,0:T(8,128)}, u32[]{:S(2)}) copy-start(f32[4,128,128]{2,1,0:T(8,128)} %get-tuple-element.5) | copy-start | bytes 786436

commit v3 on v2

--- a/solution.py
+++ b/solution.py
@@ -114,10 +114,6 @@
         load.start()
 
     barrier = pltpu.get_barrier_semaphore()
-    for step in range(1, owners):
-        pl.semaphore_signal(
-            barrier, inc=1, device_id=((me + step) % owners, band), device_id_type=MESH
-        )
     for step in range(4):
         for side in (east_band, west_band):
             pl.semaphore_signal(
@@ -126,6 +122,10 @@
                 device_id=(base + (inner + step) % 4, side),
                 device_id_type=MESH,
             )
+    for step in range(1, owners):
+        pl.semaphore_signal(
+            barrier, inc=1, device_id=((me + step) % owners, band), device_id_type=MESH
+        )
 
     table[...] = jnp.zeros_like(table)
     table[0:blocks, 0:8] = (neigh[...] + 1).astype(jnp.float32)
@@ -199,15 +199,6 @@
     edge_cols[0] = col_coefs[10 * slots : 12 * slots, :]
 
     def send_tables():
-        for step in range(1, owners):
-            pltpu.make_async_remote_copy(
-                src_ref=table,
-                dst_ref=band_tables.at[owners - step],
-                send_sem=row_send.at[SWEEPS],
-                recv_sem=row_recv.at[SWEEPS],
-                device_id=((me + step) % owners, band),
-                device_id_type=MESH,
-            ).start()
         for step in range(4):
             for slot, side in ((step, west_band), (4 + step, east_band)):
                 pltpu.make_async_remote_copy(
@@ -218,17 +209,17 @@
                     device_id=(base + (inner + step) % 4, side),
                     device_id_type=MESH,
                 ).start()
-
-    def send_edges(k):
         for step in range(1, owners):
             pltpu.make_async_remote_copy(
-                src_ref=edge_rows.at[k],
-                dst_ref=band_rows.at[k, owners - step],
-                send_sem=row_send.at[k],
-                recv_sem=row_recv.at[k],
+                src_ref=table,
+                dst_ref=band_tables.at[owners - step],
+                send_sem=row_send.at[SWEEPS],
+                recv_sem=row_recv.at[SWEEPS],
                 device_id=((me + step) % owners, band),
                 device_id_type=MESH,
             ).start()
+
+    def send_cols(k):
         for step in range(4):
             for slot, part, side in ((step, slots, west_band), (4 + step, 0, east_band)):
                 pltpu.make_async_remote_copy(
@@ -239,6 +230,17 @@
                     device_id=(base + (inner + step) % 4, side),
                     device_id_type=MESH,
                 ).start()
+
+    def send_rows(k):
+        for step in range(1, owners):
+            pltpu.make_async_remote_copy(
+                src_ref=edge_rows.at[k],
+                dst_ref=band_rows.at[k, owners - step],
+                send_sem=row_send.at[k],
+                recv_sem=row_recv.at[k],
+                device_id=((me + step) % owners, band),
+                device_id_type=MESH,
+            ).start()
         band_rows[k, 0] = edge_rows[k]
 
     def take(ref, sem):
@@ -288,7 +290,6 @@
             pick_cols[2 * slots * i : 2 * slots * (i + 1), :] = jnp.where(good, 1.0, 0.0)
 
     def take_edges(k):
-        now = k % 2
         take(band_rows.at[k, pl.ds(1, owners - 1)], row_recv.at[k])
         per_tile = width // (2 * slots)
         got = jnp.zeros((2 * slots, width), jnp.float32)
@@ -299,9 +300,6 @@
                 precision=EXACT,
                 preferred_element_type=jnp.float32,
             )
-        for s in range(slots):
-            field[now, s, PAD - 1 : PAD, :] = got[s : s + 1, :]
-            field[now, s, PAD + height : PAD + height + 1, :] = got[slots + s : slots + s + 1, :]
         take(side_cols.at[k], col_recv.at[k])
         count = 8 * slots
         cols = jnp.dot(
@@ -315,12 +313,19 @@
         above = jnp.where(lanes == width - 1, cols[2 * slots : 4 * slots], straight)
         below = jnp.where(lanes == 0, cols[4 * slots : 6 * slots], straight)
         slanted = pltpu.roll(above, 1, 1) + pltpu.roll(below, width - 1, 1)
+        return got, straight, slanted
+
+    def put_halo(k, got, straight, slanted):
+        now = k % 2
+        for s in range(slots):
+            field[now, s, PAD - 1 : PAD, :] = got[s : s + 1, :]
+            field[now, s, PAD + height : PAD + height + 1, :] = got[slots + s : slots + s + 1, :]
         for i, tile in enumerate((straight, slanted)):
             for h in range(2):
                 filled[pl.ds(2 * slots * i + h, slots, stride=2), :] = tile[
                     slots * h : slots * (h + 1)
                 ]
-        return got, straight, slanted
+        halo_cols[...] = filled[...].T
 
     def stencil(coefs, center, level, vertical, slant):
         cx, cy, cd, inv, src = (coefs[i] for i in range(5))
@@ -341,6 +346,24 @@
         def ends(tile, at):
             part = tile[at : at + slots]
             return jnp.concatenate([part[:, 0:1], part[:, width - 1 : width]], axis=0)
+
+        def sides(at, deep):
+            part = got[at : at + slots]
+            last = width - 1 - deep
+            return jnp.concatenate([part[:, last : last + 1], part[:, deep : deep + 1]], axis=0)
+
+        center = edge_cols[k]
+        inside = inner_cols[...]
+        level = inside + straight
+        vertical = spread(center, sides(0, 0), sides(slots, 0))
+        slant = slanted + spread(inside, sides(0, 1), sides(slots, 1))
+        tall = 2 * slots
+        coefs = [col_coefs[i * tall : (i + 1) * tall, :] for i in range(5)]
+        left = stencil(coefs, center, level, vertical, slant)
+        change = weight * left + keep * col_coefs[5 * tall : 6 * tall, :]
+        col_coefs[5 * tall : 6 * tall, :] = change
+        edge_cols[k + 1] = center + change
+        send_cols(k + 1)
 
         center = edge_rows[k]
         inside = jnp.concatenate(
@@ -355,30 +378,14 @@
         change = weight * left + keep * row_coefs[5]
         row_coefs[5] = change
         edge_rows[k + 1] = center + change
-
-        def sides(at, deep):
-            part = got[at : at + slots]
-            last = width - 1 - deep
-            return jnp.concatenate([part[:, last : last + 1], part[:, deep : deep + 1]], axis=0)
-
-        center = edge_cols[k]
-        inside = inner_cols[...]
-        level = inside + straight
-        vertical = spread(center, sides(0, 0), sides(slots, 0))
-        slant = slanted + spread(inside, sides(0, 1), sides(slots, 1))
-        tall = 2 * slots
-        coefs = [col_coefs[i * tall : (i + 1) * tall, :] for i in range(5)]
-        left = stencil(coefs, center, level, vertical, slant)
-        change = weight * left + keep * col_coefs[5 * tall : 6 * tall, :]
-        col_coefs[5 * tall : 6 * tall, :] = change
-        edge_cols[k + 1] = center + change
+        send_rows(k + 1)
 
     def around(value, halo):
         left = jnp.where(first_lane, halo, pltpu.roll(value, 1, 1))
         right = jnp.where(last_lane, halo, pltpu.roll(value, width - 1, 1))
         return left + right
 
-    def sweep(k):
+    def sweep(k, first, stop):
         now = k % 2
 
         def one(s, carry):
@@ -409,8 +416,7 @@
                     put_columns(0, s, r0, fresh, 1)
             return carry
 
-        halo_cols[...] = filled[...].T
-        lax.fori_loop(0, slots, one, 0)
+        lax.fori_loop(first, stop, one, 0)
         if k < SWEEPS - 1:
             inner_cols[...] = col_tile[...].T[0 : 2 * slots]
 
@@ -497,17 +503,18 @@
 
     pl.semaphore_wait(barrier, owners - 1 + 8)
     send_tables()
-    send_edges(0)
+    send_cols(0)
+    send_rows(0)
     build_picks()
-    for k in range(SWEEPS):
-        if k == SWEEPS - 1:
-            start_move(0)
-            cross_move(0)
+    for k in range(SWEEPS - 1):
         halo = take_edges(k)
-        if k < SWEEPS - 1:
-            ring(k, *halo)
-            send_edges(k + 1)
-        sweep(k)
+        ring(k, *halo)
+        put_halo(k, *halo)
+        sweep(k, 0, slots)
+    start_move(0)
+    cross_move(0)
+    put_halo(SWEEPS - 1, *take_edges(SWEEPS - 1))
+    sweep(SWEEPS - 1, 0, slots)
     start_move(1)
     cross_move(1)
     finish_move(0, sol_out)

time: 43.9 us -> 43.5 us (level)
  Pallas kernels: 40.7 us -> 40.2 us
    pallas_call x1, Pallas kernels: 40.7 us -> 40.2 us  [per_device(): pl.pallas_call(functools.partial(kernel, owners, bands), out_shape=(out,...]
where the time goes in v3:
time: 43.5 us; the launch traced here: 43.3 us
  Pallas kernels  40.2 us (92%)
  local copies, waits for them, and re-layouts  2.42 us (6%)
  between operations  0.65 us (1%)
    pallas_call x1, Pallas kernels, per_device(): pl.pallas_call(functools.partial(kernel, owners, bands), out_shape=(out,...  40.2 us
    unnamed x4, local copies, waits for them, and re-layouts  2.42 us

profile of v3, /device:TPU:0, one launch (start us, length us, event | category | flops | bytes accessed | tf_op | source)
XLA Modules:
  0.0 43.3 jit_solution(2984052995943593275)
XLA Ops:
  0.6 40.2 %barotropic_solve.1 = (f32[4,128,128]{2,1,0:T(8,128)}, f32[4,128,128]{2,1,0:T(8,128)}) custom-call(f32[8,128,128]{2,1,0:T(8,128)} %depth_hbm.1, f32[8,128,128]{2,1,0:T(8,128)} %dx_hbm.1, f32[8,128,128]{2,1,0:T(8,128)} %dy_hbm.1, f32[8,128,128]{2,1,0:T(8,128)} %forcing_hbm.1, s32[8,128,128]{2,1,0:T(8,128)} %mask_hbm.1, s32[8]{0:T(128)} %dest_smem.1, ...), custom_call_target="tpu_custom_call" | custom-call | tf_op jit(solution)/shard_map/barotropic_solve/pallas_call | solution.py:547
  40.9 0.0 copy-start
  40.9 1.7 %copy.11 = f32[4,128,128]{2,1,0:T(8,128)} copy(f32[4,128,128]{2,1,0:T(8,128)} %get-tuple-element.4) | data formatting | bytes 524288
  42.6 0.0 copy-done
  42.6 0.7 %copy.12 = f32[4,128,128]{2,1,0:T(8,128)} copy(f32[4,128,128]{2,1,0:T(8,128)S(1)} %copy-done) | data formatting | bytes 524288
Async XLA Ops:
  40.9 1.7 %copy-start = (f32[4,128,128]{2,1,0:T(8,128)S(1)}, f32[4,128,128]{2,1,0:T(8,128)}, u32[]{:S(2)}) copy-start(f32[4,128,128]{2,1,0:T(8,128)} %get-tuple-element.5) | copy-start | bytes 786436
